TPU v7x, 256 devices: a whole 4x4x8 slice. The times are simulated.
256 devices in a mesh: row: 32 (over z, y_lo, core), col: 8 (over x, y_hi).
Axes of the slice: x: 4, y: 4 (y_hi: 2, y_lo: 2; y = y_hi * 2 + y_lo), z: 8, core: 2. Of those that a mesh axis runs over, the one named last changes fastest.
Arguments:
- activations: bfloat16 [1024, 16384], P('col', 'row'), may hold values from -6 to 6
- out_grad: bfloat16 [1024, 16384], P('col', 'row'), may hold values from -2 to 2
- gate_pre: bfloat16 [1024, 8192], P('row', 'col'), may hold values from -6 to 6
- up_pre: bfloat16 [1024, 8192], P('row', 'col'), may hold values from -6 to 6
- gate_weight: bfloat16 [16384, 8192], P('row', 'col'), may hold values from -0.046875 to 0.046875
- up_weight: bfloat16 [16384, 8192], P('row', 'col'), may hold values from -0.046875 to 0.046875
- down_weight: bfloat16 [8192, 16384], P('col', 'row'), may hold values from -0.0625 to 0.0625
Outputs:
- input_grad: bfloat16 [1024, 16384], P('col', 'row')
- gate_grad: bfloat16 [16384, 8192], P('row', 'col')
- up_grad: bfloat16 [16384, 8192], P('row', 'col')
- down_grad: bfloat16 [8192, 16384], P('col', 'row')
All inputs are finite; a program needn't handle non-finite values.
Results may differ from a plain program's by a relative error of at most 0.0051.
Values may be sent and summed in bfloat16 or wider, within the bound.
A program may use at most 64 MiB of HBM per device.

v0:
```python
import jax
import jax.numpy as jnp
from jax import lax
from jax.sharding import PartitionSpec as P


def contract_rows(left, right):
    return lax.dot_general(
        left, right, (((0,), (0,)), ((), ())), preferred_element_type=jnp.float32
    )


def contract_cols(left, right):
    return lax.dot_general(
        left, right, (((1,), (1,)), ((), ())), preferred_element_type=jnp.float32
    )


def derive(hidden_grad, gate_pre, up_pre):
    gate_val = gate_pre.astype(jnp.float32)
    up_val = up_pre.astype(jnp.float32)
    gate_sig = jax.nn.sigmoid(gate_val)
    swish_val = gate_val * gate_sig
    hidden = (swish_val * up_val).astype(jnp.bfloat16)
    gate_back = (hidden_grad * up_val * gate_sig * (1.0 + gate_val * (1.0 - gate_sig))).astype(
        jnp.bfloat16
    )
    up_back = (hidden_grad * swish_val).astype(jnp.bfloat16)
    return (hidden, gate_back, up_back)


def per_device(activations, out_grad, gate_pre, up_pre, gate_weight, up_weight, down_weight):
    acts_all, grad_all = (
        lax.all_gather(activations, "col", axis=0, tiled=True),
        lax.all_gather(out_grad, "col", axis=0, tiled=True),
    )
    grad_rows = grad_all
    hidden_grad = lax.psum_scatter(
        contract_cols(grad_rows, down_weight), "row", scatter_dimension=0, tiled=True
    )
    hidden, gate_back, up_back = derive(hidden_grad, gate_pre, up_pre)
    hid_piece = lax.all_gather(hidden, "row", axis=0, tiled=True)
    gate_piece = lax.all_gather(gate_back, "row", axis=0, tiled=True)
    up_piece = lax.all_gather(up_back, "row", axis=0, tiled=True)
    grad_rows = grad_all
    down_acc = contract_rows(hid_piece, grad_rows)
    gate_acc = contract_rows(acts_all, gate_piece)
    up_acc = contract_rows(acts_all, up_piece)
    input_rows = contract_cols(gate_piece, gate_weight) + contract_cols(up_piece, up_weight)
    input_acc = input_rows
    down_acc, gate_acc, up_acc, input_acc = (down_acc, gate_acc, up_acc, input_acc)
    input_grad = lax.psum_scatter(input_acc, "col", scatter_dimension=0, tiled=True)
    return (
        input_grad.astype(jnp.bfloat16),
        gate_acc.astype(jnp.bfloat16),
        up_acc.astype(jnp.bfloat16),
        down_acc.astype(jnp.bfloat16),
    )


def solution(mesh):
    placed = (
        P("col", "row"),
        P("col", "row"),
        P("row", "col"),
        P("row", "col"),
        P("row", "col"),
        P("row", "col"),
        P("col", "row"),
    )
    return jax.shard_map(
        per_device,
        mesh=mesh,
        in_specs=placed,
        out_specs=(P("col", "row"), P("row", "col"), P("row", "col"), P("col", "row")),
        check_vma=False,
    )
```

profile of v0, /device:TPU:32, one launch (start us, length us, event | category | flops | bytes accessed | tf_op | source)
XLA Modules:
  0.0 538.8 jit_solution(6172015009212809988)
XLA Ops:
  7.2 0.0 copy-start
  7.2 0.0 all-gather.6.cloned.1.call-start
  7.2 0.7 all-gather.6.cloned.1.call-update
  7.9 0.0 reduce-scatter.3.cloned.1.call-start
  8.0 57.5 %all-gather.6.cloned.1.call-done = bf16[1024,512]{1,0:T(8,128)(2,1)} async-done(((bf16[128,512]{1,0:T(8,128)(2,1)}), bf16[1024,512]{1,0:T(8,128)(2,1)}) %all-gather.6.cloned.1.call-update) | async-done | bytes 1048592 | tf_op jit(solution)/shard_map/all_gather | solution.py:35
  65.5 0.0 copy-done
  65.5 4.4 fusion.10
  69.9 0.0 copy-start.1
  69.9 0.0 copy-start.2
  70.0 0.0 copy-start.3
  70.0 0.0 reduce-scatter.3.cloned.1.call-update
  70.0 0.0 all-gather.8.cloned.1.call-start
  70.0 117.0 %reduce-scatter.3.cloned.1.call-done = f32[32,1024]{1,0:T(8,128)} async-done(((f32[1024,1024]{1,0:T(8,128)}), f32[32,1024]{1,0:T(8,128)}) %reduce-scatter.3.cloned.1.call-update) | async-done | bytes 131088 | tf_op jit(solution)/shard_map/reduce_scatter | solution.py:38
  187.1 0.0 copy-done.1
  187.1 0.0 copy-done.2
  187.1 1.6 multiply_convert_fusion
  188.7 0.0 all-gather.8.cloned.1.call-update
  188.7 0.0 all-gather.10.cloned.1.call-start
  188.8 0.5 all-gather.10.cloned.1.call-update
  189.3 0.0 all-gather.12.cloned.1.call-start
  189.4 0.5 all-gather.12.cloned.1.call-update
  189.9 0.0 all-gather.14.cloned.1.call-start
  189.9 0.5 all-gather.14.cloned.1.call-update
  190.5 0.0 copy-start.4
  190.5 0.0 reduce-scatter.5.cloned.1.call-start
  190.5 67.7 %all-gather.8.cloned.1.call-done = bf16[1024,1024]{1,0:T(8,128)(2,1)} async-done(((bf16[32,1024]{1,0:T(8,128)(2,1)}), bf16[1024,1024]{1,0:T(8,128)(2,1)}) %all-gather.8.cloned.1.call-update) | async-done | bytes 2097168 | tf_op jit(solution)/shard_map/all_gather | solution.py:43
  258.2 0.0 copy-done.3
  258.2 4.2 fusion.11
  262.5 62.1 %all-gather.10.cloned.1.call-done = bf16[1024,1024]{1,0:T(8,128)(2,1)} async-done(((bf16[32,1024]{1,0:T(8,128)(2,1)}), bf16[1024,1024]{1,0:T(8,128)(2,1)}) %all-gather.10.cloned.1.call-update) | async-done | bytes 2097168 | tf_op jit(solution)/shard_map/all_gather | solution.py:44
  324.5 0.0 copy-done.4
  324.5 4.9 convolution_add_fusion
  329.4 0.0 reduce-scatter.5.cloned.1.call-update
  329.5 50.4 %all-gather.12.cloned.1.call-done = bf16[1024,512]{1,0:T(8,128)(2,1)} async-done(((bf16[128,512]{1,0:T(8,128)(2,1)}), bf16[1024,512]{1,0:T(8,128)(2,1)}) %all-gather.12.cloned.1.call-update) | async-done | bytes 1048592 | tf_op jit(solution)/shard_map/all_gather | solution.py:34
  379.9 3.1 fusion
  383.0 0.0 copy-start.6
  383.0 1.3 copy.11
  384.3 0.0 copy-done.6
  384.3 2.9 fusion.1
  387.2 0.0 copy-start.5
  387.2 1.3 copy.12
  388.6 55.5 %all-gather.14.cloned.1.call-done = bf16[1024,1024]{1,0:T(8,128)(2,1)} async-done(((bf16[32,1024]{1,0:T(8,128)(2,1)}), bf16[1024,1024]{1,0:T(8,128)(2,1)}) %all-gather.14.cloned.1.call-update) | async-done | bytes 2097168 | tf_op jit(solution)/shard_map/all_gather | solution.py:42
  444.0 0.0 copy-done.5
  444.0 3.8 convolution_convert_fusion
  447.9 82.5 %reduce-scatter.5.cloned.1.call-done = f32[128,512]{1,0:T(8,128)} async-done(((f32[1024,512]{1,0:T(8,128)}), f32[128,512]{1,0:T(8,128)}) %reduce-scatter.5.cloned.1.call-update) | async-done | bytes 262160 | tf_op jit(solution)/shard_map/reduce_scatter | solution.py:52
  530.4 1.6 convert_element_type.37
Async XLA Ops:
  7.2 58.3 %copy-start = (bf16[1024,512]{1,0:T(8,128)(2,1)S(1)}, bf16[1024,512]{1,0:T(8,128)(2,1)}, u32[]{:S(2)}) copy-start(bf16[1024,512]{1,0:T(8,128)(2,1)} %param.13) | copy-start | bytes 3145732
  7.2 58.3 %all-gather.6.cloned.1.call-start = ((), (), s32[]{:S(2)}) async-start(), calls=%async_computation.2 | async-start | bytes 1179648 | tf_op jit(solution)/shard_map/all_gather | solution.py:35
  7.9 179.1 %reduce-scatter.3.cloned.1.call-start = ((), (), s32[]{:S(2)}) async-start(), calls=%async_computation.3 | async-start | bytes 4325376 | tf_op jit(solution)/shard_map/reduce_scatter | solution.py:38
  69.9 117.1 %copy-start.1 = (bf16[32,1024]{1,0:T(8,128)(2,1)S(1)}, bf16[32,1024]{1,0:T(8,128)(2,1)}, u32[]{:S(2)}) copy-start(bf16[32,1024]{1,0:T(8,128)(2,1)} %param.9) | copy-start | bytes 196612
  69.9 117.1 %copy-start.2 = (bf16[32,1024]{1,0:T(8,128)(2,1)S(1)}, bf16[32,1024]{1,0:T(8,128)(2,1)}, u32[]{:S(2)}) copy-start(bf16[32,1024]{1,0:T(8,128)(2,1)} %param.10) | copy-start | bytes 196612
  70.0 188.3 %copy-start.3 = (bf16[512,1024]{1,0:T(8,128)(2,1)S(1)}, bf16[512,1024]{1,0:T(8,128)(2,1)}, u32[]{:S(2)}) copy-start(bf16[512,1024]{1,0:T(8,128)(2,1)} %param.11) | copy-start | bytes 3145732
  70.0 188.2 %all-gather.8.cloned.1.call-start = ((), (), s32[]{:S(2)}) async-start(), calls=%async_computation.4 | async-start | bytes 2162688 | tf_op jit(solution)/shard_map/all_gather | solution.py:43
  188.7 135.8 %all-gather.10.cloned.1.call-start = ((), (), s32[]{:S(2)}) async-start(), calls=%async_computation.5 | async-start | bytes 2162688 | tf_op jit(solution)/shard_map/all_gather | solution.py:44
  189.3 190.6 %all-gather.12.cloned.1.call-start = ((), (), s32[]{:S(2)}) async-start(), calls=%async_computation.7 | async-start | bytes 1179648 | tf_op jit(solution)/shard_map/all_gather | solution.py:34
  189.9 254.2 %all-gather.14.cloned.1.call-start = ((), (), s32[]{:S(2)}) async-start(), calls=%async_computation.8 | async-start | bytes 2162688 | tf_op jit(solution)/shard_map/all_gather | solution.py:42
  190.5 134.1 %copy-start.4 = (bf16[512,1024]{1,0:T(8,128)(2,1)S(1)}, bf16[512,1024]{1,0:T(8,128)(2,1)}, u32[]{:S(2)}) copy-start(bf16[512,1024]{1,0:T(8,128)(2,1)} %param.12) | copy-start | bytes 3145732
  190.5 339.9 %reduce-scatter.5.cloned.1.call-start = ((), (), s32[]{:S(2)}) async-start(), calls=%async_computation.6 | async-start | bytes 2359296 | tf_op jit(solution)/shard_map/reduce_scatter | solution.py:52
  383.0 1.3 copy-start.6
  387.2 56.8 %copy-start.5 = (bf16[1024,512]{1,0:T(8,128)(2,1)S(1)}, bf16[1024,512]{1,0:T(8,128)(2,1)}, u32[]{:S(2)}) copy-start(bf16[1024,512]{1,0:T(8,128)(2,1)} %all-gather.6.cloned.1.call-done) | copy-start | bytes 3145732
Sparse Core Ops, SparseCore 0:
  10.6 54.8 all-gather.5
  70.1 116.9 reduce-scatter.2
  189.5 68.6 all-gather.7
  260.5 63.9 all-gather.9
  327.0 52.8 all-gather.11
  381.6 62.4 all-gather.13
  448.1 82.2 reduce-scatter.4
where the time goes:
time: 539 us
  waiting for transfers between devices  495 us (92%)
  matrix products  23.4 us (4%)
  between operations  14.2 us (3%)
    reduce_scatter x1, waiting for transfers between devices, per_device(): lax.psum_scatter(contract_cols(grad_rows, down_weight), 'row', scatter_di...  117 us
    reduce_scatter x1, waiting for transfers between devices, per_device(): lax.psum_scatter(input_acc, 'col', scatter_dimension=0, tiled=True)  82.5 us
    all_gather x1, waiting for transfers between devices, per_device(): gate_piece = lax.all_gather(gate_back, 'row', axis=0, tiled=True)  67.7 us
    all_gather x1, waiting for transfers between devices, per_device(): up_piece = lax.all_gather(up_back, 'row', axis=0, tiled=True)  62.1 us
    all_gather x1, waiting for transfers between devices, per_device(): lax.all_gather(out_grad, 'col', axis=0, tiled=True)  57.5 us
    all_gather x1, waiting for transfers between devices, per_device(): hid_piece = lax.all_gather(hidden, 'row', axis=0, tiled=True)  55.5 us
    all_gather x1, waiting for transfers between devices, per_device(): lax.all_gather(activations, 'col', axis=0, tiled=True)  50.4 us
    dot_general x3, matrix products, contract_cols(): lax.dot_general(left, right, (((1,), (1,)), ((), ())), preferred_element_...  13.6 us
  transfers between devices with their start and end apart: 7, of which 7 were waited for; matrix products, arithmetic and copies ran while one was open for 4% of the time, Pallas kernels for 0%

commit v1 on v0

--- a/solution.py
+++ b/solution.py
@@ -41,7 +41,9 @@
     hidden, gate_back, up_back = derive(hidden_grad, gate_pre, up_pre)
     hid_piece = lax.all_gather(hidden, "row", axis=0, tiled=True)
     gate_piece = lax.all_gather(gate_back, "row", axis=0, tiled=True)
-    up_piece = lax.all_gather(up_back, "row", axis=0, tiled=True)
+    up_piece = jnp.concatenate(
+        lax.all_to_all(jnp.stack([up_back] * lax.axis_size("row")), "row", 0, 0), axis=0
+    )
     grad_rows = grad_all
     down_acc = contract_rows(hid_piece, grad_rows)
     gate_acc = contract_rows(acts_all, gate_piece)

time: 539 us -> 488 us (0.905)
  waiting for transfers between devices: 495 us -> 428 us
  starting transfers between devices: 0.27 us -> 12.3 us
    all_gather x1 -> x0, waiting for transfers between devices: 62.1 us -> none  [per_device(): up_piece = lax.all_gather(up_back, 'row', axis=0, tiled=True)]
    all_to_all x0 -> x1, starting transfers between devices: none -> 12.1 us  [per_device(): lax.all_to_all(jnp.stack([up_back] * lax.axis_size('row')), 'row', 0, 0)]
  transfers between devices with their start and end apart: 7 -> 7, of which waited for: 7 -> 6; matrix products, arithmetic and copies ran while one was open for 4% -> 5% of each run, Pallas kernels for 0% -> 0%
where the time goes in v1:
time: 488 us; the launch traced here: 487 us
  waiting for transfers between devices  428 us (88%)
  matrix products  23.7 us (5%)
  between operations  14.2 us (3%)
  starting transfers between devices  12.3 us (3%)
  local copies, waits for them, and re-layouts  5.31 us (1%)
    reduce_scatter x1, waiting for transfers between devices, per_device(): lax.psum_scatter(contract_cols(grad_rows, down_weight), 'row', scatter_di...  117 us
    reduce_scatter x1, waiting for transfers between devices, per_device(): lax.psum_scatter(input_acc, 'col', scatter_dimension=0, tiled=True)  82.3 us
    all_gather x1, waiting for transfers between devices, per_device(): gate_piece = lax.all_gather(gate_back, 'row', axis=0, tiled=True)  68.5 us
    all_gather x1, waiting for transfers between devices, per_device(): lax.all_gather(out_grad, 'col', axis=0, tiled=True)  57.5 us
    all_gather x1, waiting for transfers between devices, per_device(): hid_piece = lax.all_gather(hidden, 'row', axis=0, tiled=True)  54.1 us
    all_gather x1, waiting for transfers between devices, per_device(): lax.all_gather(activations, 'col', axis=0, tiled=True)  47.1 us
    dot_general x3, matrix products, contract_cols(): lax.dot_general(left, right, (((1,), (1,)), ((), ())), preferred_element_...  13.5 us
    all_to_all x1, starting transfers between devices, per_device(): lax.all_to_all(jnp.stack([up_back] * lax.axis_size('row')), 'row', 0, 0)  12.1 us
  transfers between devices with their start and end apart: 7, of which 6 were waited for; matrix products, arithmetic and copies ran while one was open for 5% of the time, Pallas kernels for 0%

profile of v1, /device:TPU:32, one launch (start us, length us, event | category | flops | bytes accessed | tf_op | source)
XLA Modules:
  0.0 487.1 jit_solution(15038869222550834632)
XLA Ops:
  7.2 0.0 copy-start
  7.2 0.0 all-gather.5.cloned.1.call-start
  7.2 0.7 all-gather.5.cloned.1.call-update
  7.9 0.0 reduce-scatter.3.cloned.1.call-start
  8.0 57.5 %all-gather.5.cloned.1.call-done = bf16[1024,512]{1,0:T(8,128)(2,1)} async-done(((bf16[128,512]{1,0:T(8,128)(2,1)}), bf16[1024,512]{1,0:T(8,128)(2,1)}) %all-gather.5.cloned.1.call-update) | async-done | bytes 1048592 | tf_op jit(solution)/shard_map/all_gather | solution.py:35
  65.5 0.0 copy-done
  65.5 4.5 fusion.10
  70.0 0.0 copy-start.1
  70.0 0.0 copy-start.2
  70.0 0.0 reduce-scatter.3.cloned.1.call-update
  70.0 0.0 all-gather.7.cloned.1.call-start
  70.0 117.1 %reduce-scatter.3.cloned.1.call-done = f32[32,1024]{1,0:T(8,128)} async-done(((f32[1024,1024]{1,0:T(8,128)}), f32[32,1024]{1,0:T(8,128)}) %reduce-scatter.3.cloned.1.call-update) | async-done | bytes 131088 | tf_op jit(solution)/shard_map/reduce_scatter | solution.py:38
  187.1 0.0 copy-done.1
  187.1 0.0 copy-done.2
  187.1 1.6 multiply_convert_fusion
  188.7 0.0 all-gather.7.cloned.1.call-update
  188.8 0.0 all-gather.9.cloned.1.call-start
  188.8 0.5 all-gather.9.cloned.1.call-update
  189.4 1.6 stack.2
  191.0 12.1 %all-to-all-start = ((bf16[32,32,1024]{2,1,0:T(8,128)(2,1)}), bf16[32,32,1024]{2,1,0:T(8,128)(2,1)S(1)}, u32[]{:S(2)}, u32[]{:S(2)}) async-start(bf16[32,32,1024]{2,1,0:T(8,128)(2,1)} %stack.2), calls=%async_computation.1 | async-start | bytes 4194304 | tf_op jit(solution)/shard_map/all_to_all | solution.py:45
  203.1 0.0 all-gather.11.cloned.1.call-start
  203.1 0.5 all-gather.11.cloned.1.call-update
  203.7 0.0 reduce-scatter.5.cloned.1.call-start
  203.7 68.5 %all-gather.7.cloned.1.call-done = bf16[1024,1024]{1,0:T(8,128)(2,1)} async-done(((bf16[32,1024]{1,0:T(8,128)(2,1)}), bf16[1024,1024]{1,0:T(8,128)(2,1)}) %all-gather.7.cloned.1.call-update) | async-done | bytes 2097168 | tf_op jit(solution)/shard_map/all_gather | solution.py:43
  272.2 4.5 fusion.11
  276.7 0.0 all-to-all-done
  276.7 4.6 convolution_add_fusion
  281.2 0.0 reduce-scatter.5.cloned.1.call-update
  281.3 47.1 %all-gather.9.cloned.1.call-done = bf16[1024,512]{1,0:T(8,128)(2,1)} async-done(((bf16[128,512]{1,0:T(8,128)(2,1)}), bf16[1024,512]{1,0:T(8,128)(2,1)}) %all-gather.9.cloned.1.call-update) | async-done | bytes 1048592 | tf_op jit(solution)/shard_map/all_gather | solution.py:34
  328.3 3.5 fusion.1
  331.8 0.0 copy-start.4
  331.8 2.4 copy.12
  334.1 0.0 copy-done.4
  334.1 2.9 fusion
  337.0 0.0 copy-start.3
  337.0 1.3 copy.11
  338.3 54.1 %all-gather.11.cloned.1.call-done = bf16[1024,1024]{1,0:T(8,128)(2,1)} async-done(((bf16[32,1024]{1,0:T(8,128)(2,1)}), bf16[1024,1024]{1,0:T(8,128)(2,1)}) %all-gather.11.cloned.1.call-update) | async-done | bytes 2097168 | tf_op jit(solution)/shard_map/all_gather | solution.py:42
  392.5 0.0 copy-done.3
  392.5 3.8 convolution_convert_fusion
  396.3 82.3 %reduce-scatter.5.cloned.1.call-done = f32[128,512]{1,0:T(8,128)} async-done(((f32[1024,512]{1,0:T(8,128)}), f32[128,512]{1,0:T(8,128)}) %reduce-scatter.5.cloned.1.call-update) | async-done | bytes 262160 | tf_op jit(solution)/shard_map/reduce_scatter | solution.py:54
  478.6 1.6 convert_element_type.37
Async XLA Ops:
  7.2 58.3 %copy-start = (bf16[1024,512]{1,0:T(8,128)(2,1)S(1)}, bf16[1024,512]{1,0:T(8,128)(2,1)}, u32[]{:S(2)}) copy-start(bf16[1024,512]{1,0:T(8,128)(2,1)} %param.13) | copy-start | bytes 3145732
  7.2 58.3 %all-gather.5.cloned.1.call-start = ((), (), s32[]{:S(2)}) async-start(), calls=%async_computation.3 | async-start | bytes 1179648 | tf_op jit(solution)/shard_map/all_gather | solution.py:35
  7.9 179.2 %reduce-scatter.3.cloned.1.call-start = ((), (), s32[]{:S(2)}) async-start(), calls=%async_computation.4 | async-start | bytes 4325376 | tf_op jit(solution)/shard_map/reduce_scatter | solution.py:38
  70.0 117.1 %copy-start.1 = (bf16[32,1024]{1,0:T(8,128)(2,1)S(1)}, bf16[32,1024]{1,0:T(8,128)(2,1)}, u32[]{:S(2)}) copy-start(bf16[32,1024]{1,0:T(8,128)(2,1)} %param.9) | copy-start | bytes 196612
  70.0 117.1 %copy-start.2 = (bf16[32,1024]{1,0:T(8,128)(2,1)S(1)}, bf16[32,1024]{1,0:T(8,128)(2,1)}, u32[]{:S(2)}) copy-start(bf16[32,1024]{1,0:T(8,128)(2,1)} %param.10) | copy-start | bytes 196612
  70.0 202.2 %all-gather.7.cloned.1.call-start = ((), (), s32[]{:S(2)}) async-start(), calls=%async_computation.5 | async-start | bytes 2162688 | tf_op jit(solution)/shard_map/all_gather | solution.py:43
  188.8 139.5 %all-gather.9.cloned.1.call-start = ((), (), s32[]{:S(2)}) async-start(), calls=%async_computation.7 | async-start | bytes 1179648 | tf_op jit(solution)/shard_map/all_gather | solution.py:34
  191.0 85.7 %all-to-all-start = ((bf16[32,32,1024]{2,1,0:T(8,128)(2,1)}), bf16[32,32,1024]{2,1,0:T(8,128)(2,1)S(1)}, u32[]{:S(2)}, u32[]{:S(2)}) async-start(bf16[32,32,1024]{2,1,0:T(8,128)(2,1)} %stack.2), calls=%async_computation.1 | async-start | bytes 4194304 | tf_op jit(solution)/shard_map/all_to_all | solution.py:45
  203.1 189.4 %all-gather.11.cloned.1.call-start = ((), (), s32[]{:S(2)}) async-start(), calls=%async_computation.8 | async-start | bytes 2162688 | tf_op jit(solution)/shard_map/all_gather | solution.py:42
  203.7 275.0 %reduce-scatter.5.cloned.1.call-start = ((), (), s32[]{:S(2)}) async-start(), calls=%async_computation.6 | async-start | bytes 2359296 | tf_op jit(solution)/shard_map/reduce_scatter | solution.py:54
  331.8 2.4 copy-start.4
  337.0 55.5 %copy-start.3 = (bf16[1024,512]{1,0:T(8,128)(2,1)S(1)}, bf16[1024,512]{1,0:T(8,128)(2,1)}, u32[]{:S(2)}) copy-start(bf16[1024,512]{1,0:T(8,128)(2,1)} %all-gather.5.cloned.1.call-done) | copy-start | bytes 3145732
Sparse Core Ops, SparseCore 0:
  10.6 54.8 all-gather.4
  70.1 116.9 reduce-scatter.2
  189.5 82.5 all-gather.6
  274.7 53.6 all-gather.8
  330.0 62.4 all-gather.10
  396.4 82.2 reduce-scatter.4
